TPU v7x, 32 devices: a whole 2x2x4 slice. The times are simulated.
32 devices in a mesh: group: 2 (over y), ctx: 4 (over z), feat: 2 (over x), ex: 2 (over core).
Axes of the slice: x: 2, y: 2, z: 4, core: 2. Of those that a mesh axis runs over, the one named last changes fastest.
Arguments:
- hidden: bfloat16 [8, 512, 8192], P(('group', 'feat', 'ex'), 'ctx'), parts along dimension 0, may hold values from -6 to 6
- cotangent: bfloat16 [8, 512, 1024], P(('group', 'feat', 'ex'), 'ctx'), parts along dimension 0, may hold values from -6 to 6
- adapter_down_factor: bfloat16 [8192, 16], replicated, may hold values from -0.0625 to 0.0625
- projection: bfloat16 [16384, 8192], P('ctx', 'feat'), may hold values from -6 to 6
- lengths: int32 [8], P(('group', 'feat', 'ex')), parts along dimension 0, may hold values from 128 to 512, as said below
- slot_example_order: int32 [8], P('group'), parts along dimension 0, may hold values from 0 to 3, each once
Outputs:
- features: float32 [8, 8192], P(('group', 'ex'), 'feat'), parts along dimension 0
There are 2 independent parts, one for each index of `group`. A program takes and returns all parts, laid end to end along the dimension named above; an argument that names none is the same for every part. Nothing has to cross between parts.
Inputs may be any that keep to these rules, and one draw needn't show every extreme that they name: `lengths`: some example has exactly 512 valid positions and some exactly one quarter of 512.
All inputs are finite; a program needn't handle non-finite values.
Results may differ from a plain program's by a relative error of at most 0.0042.
Values may be sent and summed in bfloat16 or wider, within the bound.
No kernel may reach another device: no remote copies, remote signals or barrier semaphores. Data moves between devices by JAX's collectives and lax.ppermute only.
A program may use at most 64 MiB of HBM per device.

v0:
```python
import jax
import jax.numpy as jnp
from jax import lax
from jax.sharding import PartitionSpec as P

FEATS = 8192


def per_device(hidden, cotangent, adapter_down_factor, projection, lengths, slot_example_order):
    ctx_count = lax.axis_size("ctx")
    feat_count = lax.axis_size("feat")
    example_groups = lax.axis_size("ex")
    example_count, token_count, model_width = hidden.shape
    down_factor_rows = jnp.dot(
        hidden.reshape(example_count * token_count, model_width),
        adapter_down_factor,
        preferred_element_type=jnp.float32,
    )
    down_factor_rows = down_factor_rows.astype(jnp.bfloat16).reshape(example_count, token_count, -1)
    position = lax.axis_index("ctx") * token_count + lax.iota(jnp.int32, token_count)
    retain_mask = (position[None, :] < lengths[:, None]).astype(jnp.bfloat16)
    down_factor_rows = down_factor_rows * retain_mask[:, :, None]
    partial_value = jnp.einsum(
        "etr,etj->erj", down_factor_rows, cotangent, preferred_element_type=jnp.float32
    )
    partial_value = partial_value.reshape(example_count, -1)
    block_size = partial_value.shape[1] // ctx_count
    summed_all = lax.psum(partial_value, "ctx")
    owned_rows = lax.dynamic_slice_in_dim(
        summed_all, lax.axis_index("ctx") * block_size, block_size, 1
    )
    grad_rows = owned_rows.astype(jnp.bfloat16)
    projected = jnp.dot(
        lax.all_gather(grad_rows, "feat", axis=0, tiled=True),
        projection,
        preferred_element_type=jnp.float32,
    )
    summed = lax.psum(projected, "ctx")
    squares = lax.psum(jnp.sum(summed * summed, axis=1), "feat")
    scaled = summed / jnp.sqrt(squares / FEATS + 1e-06)[:, None]
    everything = lax.all_gather(scaled, "ex", axis=0, tiled=True)
    arranged = jnp.transpose(
        slot_example_order.reshape(feat_count, example_groups, example_count), (1, 0, 2)
    ).reshape(-1)
    own_rows = everything.shape[0] // example_groups
    wanted = lax.axis_index("ex") * own_rows + lax.iota(jnp.int32, own_rows)
    select = (arranged[None, :] == wanted[:, None]).astype(jnp.float32)
    return jnp.dot(
        select, everything, precision=lax.Precision.HIGHEST, preferred_element_type=jnp.float32
    )


def solution(mesh):
    in_specs = (
        P(("group", "feat", "ex"), "ctx", None),
        P(("group", "feat", "ex"), "ctx", None),
        P(),
        P("ctx", "feat"),
        P(("group", "feat", "ex")),
        P("group"),
    )
    out_specs = P(("group", "ex"), "feat")
    return jax.shard_map(
        per_device, mesh=mesh, in_specs=in_specs, out_specs=out_specs, check_vma=False
    )
```

profile of v0, /device:TPU:0, one launch (start us, length us, event | category | flops | bytes accessed | tf_op | source)
XLA Modules:
  0.0 76.8 jit_solution(9681998552901455173)
XLA Ops:
  0.0 0.0 copy-start
  0.8 0.8 %copy-done = bf16[1,128,8192]{2,1,0:T(8,128)(2,1)S(1)} copy-done((bf16[1,128,8192]{2,1,0:T(8,128)(2,1)S(1)}, bf16[1,128,8192]{2,1,0:T(8,128)(2,1)}, u32[]{:S(2)}) %copy-start) | copy-done | bytes 2097176
  1.6 1.9 %convolution_bitcast_fusion = f32[1,1,16,1024]{3,2,1,0:T(8,128)S(1)} fusion(bf16[8192,16]{0,1:T(8,128)(2,1)} %param.8, bf16[1,128,8192]{2,1,0:T(8,128)(2,1)S(1)} %copy-done, bf16[1,128,1024]{2,1,0:T(8,128)(2,1)} %param.7, bf16[128]{0:T(256)(128)(2,1)S(1)} %compare_convert_fusion), kind=kOutput, calls=%fused_computation.2 | convolution fusion | flops 37752832 | bytes 2687232 | tf_op jit(solution)/shard_map/etr,etj->erj/dot_general | solution.py:23
  3.5 0.1 copy.11
  3.6 32.0 %psum.21 = bf16[1,16384]{1,0:T(2,128)(2,1)S(1)} all-reduce(f32[1,16384]{1,0:T(1,128)S(1)} %bitcast.31), channel_id=1, replica_groups=mesh['group'=2,'ctx'=4,'feat'=2,'ex'=2] {'ctx'}, use_global_device_ids=true, to_apply=%region_0.0 | all-reduce | flops 16384 | bytes 98304 | tf_op jit(solution)/shard_map/psum | solution.py:28
  35.6 4.4 %all-gather = bf16[2,1,4096]{2,1,0:T(2,128)(2,1)S(1)} all-gather(bf16[1,1,4096]{2,1,0:T(2,128)(2,1)S(1)} %convert_bitcast_fusion), channel_id=1, replica_groups=mesh['group'=2,'ctx'=4,'feat'=2,'ex'=2] {'feat'}, dimensions={0}, use_global_device_ids=true | all-gather | bytes 24576 | tf_op jit(solution)/shard_map/all_gather | solution.py:34
  40.0 0.0 copy-start.1
  40.0 12.8 %fusion.11 = f32[2,4096]{1,0:T(2,128)S(1)} fusion(bf16[4096,4096]{1,0:T(8,128)(2,1)} %param.9, bf16[2,1,4096]{2,1,0:T(2,128)(2,1)S(1)} %all-gather), kind=kOutput, calls=%fused_computation.8 | convolution fusion | flops 67108864 | bytes 33603584 | tf_op jit(solution)/shard_map/dot_general | solution.py:33
  52.8 15.8 %psum.22 = f32[2,4096]{1,0:T(2,128)S(1)} all-reduce(f32[2,4096]{1,0:T(2,128)S(1)} %fusion.11), channel_id=1, replica_groups=mesh['group'=2,'ctx'=4,'feat'=2,'ex'=2] {'ctx'}, use_global_device_ids=true, to_apply=%region_1.0 | all-reduce | flops 8192 | bytes 65536 | tf_op jit(solution)/shard_map/psum | solution.py:38
  68.6 0.1 multiply_reduce_fusion
  68.7 4.9 %psum.23 = f32[2]{0:T(128)S(1)} all-reduce(f32[2]{0:T(128)S(1)} %multiply_reduce_fusion), channel_id=1, replica_groups=mesh['group'=2,'ctx'=4,'feat'=2,'ex'=2] {'feat'}, use_global_device_ids=true, to_apply=%region_3.0 | all-reduce | flops 2 | bytes 16 | tf_op jit(solution)/shard_map/psum | solution.py:39
  73.7 0.1 divide_bitcast_fusion
  73.8 1.9 %all-gather.1 = f32[2,2,4096]{2,1,0:T(2,128)S(1)} all-gather(f32[1,2,4096]{2,1,0:T(2,128)S(1)} %divide_bitcast_fusion), channel_id=1, replica_groups=mesh['group'=2,'ctx'=4,'feat'=2,'ex'=2] {'ex'}, dimensions={0}, use_global_device_ids=true | all-gather | bytes 98304 | tf_op jit(solution)/shard_map/all_gather | solution.py:41
  75.6 0.1 reshape.45
  75.7 0.0 copy-done.1
  75.7 0.1 reshape.38
  75.8 0.1 copy.9
  75.9 0.1 eq.15
  76.0 0.9 %fusion.15 = f32[2,4096]{1,0:T(2,128)} fusion(f32[4,4096]{1,0:T(4,128)S(1)} %reshape.45, s32[4]{0:T(128)S(1)} %eq.15, s32[2]{0:T(128)S(1)} %iota_add_fusion), kind=kOutput, calls=%fused_computation.14 | convolution fusion | flops 393224 | bytes 98328 | tf_op jit(solution)/shard_map/dot_general | solution.py:48
  (4 shorter events, 0.0 us)
Async XLA Ops:
  0.0 1.6 %copy-start = (bf16[1,128,8192]{2,1,0:T(8,128)(2,1)S(1)}, bf16[1,128,8192]{2,1,0:T(8,128)(2,1)}, u32[]{:S(2)}) copy-start(bf16[1,128,8192]{2,1,0:T(8,128)(2,1)} %param.6) | copy-start | bytes 6291460
  40.0 35.7 %copy-start.1 = (s32[4]{0:T(128)S(1)}, s32[4]{0:T(128)}, u32[]{:S(2)}) copy-start(s32[4]{0:T(128)} %param.11) | copy-start | bytes 52
where the time goes:
time: 77.1 us; the launch traced here: 76.8 us
  blocking collectives  58.9 us (76%)
  matrix products  15.6 us (20%)
  local copies, waits for them, and re-layouts  1.22 us (2%)
  between operations  0.88 us (1%)
    psum x1, blocking collectives, per_device(): summed_all = lax.psum(partial_value, 'ctx')  32 us
    psum x1, blocking collectives, per_device(): summed = lax.psum(projected, 'ctx')  15.8 us
    dot_general x1, matrix products, per_device(): jnp.dot(lax.all_gather(grad_rows, 'feat', axis=0, tiled=True), projection...  12.8 us
    psum x1, blocking collectives, per_device(): squares = lax.psum(jnp.sum(summed * summed, axis=1), 'feat')  4.93 us
    all_gather x1, blocking collectives, per_device(): lax.all_gather(grad_rows, 'feat', axis=0, tiled=True)  4.41 us
    dot_general x1, matrix products, per_device(): jnp.einsum('etr,etj->erj', down_factor_rows, cotangent, preferred_element...  1.87 us
    all_gather x1, blocking collectives, per_device(): everything = lax.all_gather(scaled, 'ex', axis=0, tiled=True)  1.85 us

commit v1 on v0

--- a/solution.py
+++ b/solution.py
@@ -30,10 +30,29 @@
         summed_all, lax.axis_index("ctx") * block_size, block_size, 1
     )
     grad_rows = owned_rows.astype(jnp.bfloat16)
+
+    def records_raise(x_in, which_axis, out_dim):
+        lower, current_block, y_new = (
+            lax.axis_size(which_axis),
+            lax.axis_index(which_axis),
+            x_in.shape[out_dim],
+        )
+        m_next, moved = (x_in, 1)
+        while moved < lower:
+            m_next = jnp.concatenate(
+                [
+                    m_next,
+                    lax.ppermute(
+                        m_next, which_axis, [(q, (q - moved) % lower) for q in range(lower)]
+                    ),
+                ],
+                out_dim,
+            )
+            moved = 2 * moved
+        return jnp.roll(m_next, current_block * y_new, out_dim)
+
     projected = jnp.dot(
-        lax.all_gather(grad_rows, "feat", axis=0, tiled=True),
-        projection,
-        preferred_element_type=jnp.float32,
+        records_raise(grad_rows, "feat", 0), projection, preferred_element_type=jnp.float32
     )
     summed = lax.psum(projected, "ctx")
     squares = lax.psum(jnp.sum(summed * summed, axis=1), "feat")

time: 77.1 us -> 76.3 us (0.990)
  blocking collectives: 58.9 us -> 54.5 us
  waiting for transfers between devices: 0 us -> 2.06 us
  starting transfers between devices: 0 us -> 1.55 us
    all_gather x1 -> x0, blocking collectives: 4.41 us -> none  [per_device(): lax.all_gather(grad_rows, 'feat', axis=0, tiled=True)]
    ppermute x0 -> x1, waiting for transfers between devices: none -> 2.06 us  [records_raise(): lax.ppermute(m_next, which_axis, [(q, (q - moved) % lower) for q in range...]
    ppermute x0 -> x1, starting transfers between devices: none -> 1.55 us  [records_raise(): lax.ppermute(m_next, which_axis, [(q, (q - moved) % lower) for q in range...]
  transfers between devices with their start and end apart: 0 -> 1, of which waited for: 0 -> 1; matrix products, arithmetic and copies ran while one was open for 0% -> 0% of each run, Pallas kernels for 0% -> 0%
where the time goes in v1:
time: 76.3 us; the launch traced here: 76.1 us
  blocking collectives  54.5 us (71%)
  matrix products  15.6 us (20%)
  waiting for transfers between devices  2.06 us (3%)
  starting transfers between devices  1.55 us (2%)
  local copies, waits for them, and re-layouts  1.21 us (2%)
  between operations  0.86 us (1%)
    psum x1, blocking collectives, per_device(): summed_all = lax.psum(partial_value, 'ctx')  32 us
    psum x1, blocking collectives, per_device(): summed = lax.psum(projected, 'ctx')  15.8 us
    dot_general x1, matrix products, per_device(): jnp.dot(records_raise(grad_rows, 'feat', 0), projection, preferred_elemen...  12.8 us
    psum x1, blocking collectives, per_device(): squares = lax.psum(jnp.sum(summed * summed, axis=1), 'feat')  4.91 us
    ppermute x1, waiting for transfers between devices, records_raise(): lax.ppermute(m_next, which_axis, [(q, (q - moved) % lower) for q in range...  2.06 us
    dot_general x1, matrix products, per_device(): jnp.einsum('etr,etj->erj', down_factor_rows, cotangent, preferred_element...  1.93 us
    all_gather x1, blocking collectives, per_device(): everything = lax.all_gather(scaled, 'ex', axis=0, tiled=True)  1.85 us
    ppermute x1, starting transfers between devices, records_raise(): lax.ppermute(m_next, which_axis, [(q, (q - moved) % lower) for q in range...  1.55 us
  transfers between devices with their start and end apart: 1, of which 1 were waited for; matrix products, arithmetic and copies ran while one was open for 0% of the time, Pallas kernels for 0%

profile of v1, /device:TPU:0, one launch (start us, length us, event | category | flops | bytes accessed | tf_op | source)
XLA Modules:
  0.0 76.1 jit_solution(12623639687400430393)
XLA Ops:
  0.0 0.0 copy-start
  0.0 0.0 copy-start.1
  0.8 0.8 %copy-done = bf16[1,128,8192]{2,1,0:T(8,128)(2,1)S(1)} copy-done((bf16[1,128,8192]{2,1,0:T(8,128)(2,1)S(1)}, bf16[1,128,8192]{2,1,0:T(8,128)(2,1)}, u32[]{:S(2)}) %copy-start) | copy-done | bytes 2097176
  1.6 1.9 %convolution_bitcast_fusion = f32[1,1,16,1024]{3,2,1,0:T(8,128)S(1)} fusion(bf16[8192,16]{0,1:T(8,128)(2,1)} %param.8, bf16[1,128,8192]{2,1,0:T(8,128)(2,1)S(1)} %copy-done, bf16[1,128,1024]{2,1,0:T(8,128)(2,1)} %param.7, bf16[128]{0:T(256)(128)(2,1)S(1)} %compare_convert_fusion), kind=kOutput, calls=%fused_computation.2 | convolution fusion | flops 37752832 | bytes 2687232 | tf_op jit(solution)/shard_map/etr,etj->erj/dot_general | solution.py:23
  3.5 0.1 copy.9
  3.6 32.0 %psum.21 = bf16[1,16384]{1,0:T(2,128)(2,1)S(1)} all-reduce(f32[1,16384]{1,0:T(1,128)S(1)} %bitcast.26), channel_id=1, replica_groups=mesh['group'=2,'ctx'=4,'feat'=2,'ex'=2] {'ctx'}, use_global_device_ids=true, to_apply=%region_0.0 | all-reduce | flops 16384 | bytes 98304 | tf_op jit(solution)/shard_map/psum | solution.py:28
  35.6 1.6 %collective-permute-start = (bf16[1,4096]{1,0:T(2,128)(2,1)S(1)}, bf16[1,4096]{1,0:T(2,128)(2,1)S(1)}, u32[]{:S(2)}, u32[]{:S(2)}) collective-permute-start(bf16[1,4096]{1,0:T(2,128)(2,1)S(1)} %dynamic-slice_convert_fusion), channel_id=1, source_target_pairs={{0,2},{2,0},{1,3},{3,1},{4,6},{6,4},{5,7},{7,5},{8,10},{10,8},{9,1... | collective-permute-start | bytes 24584 | tf_op jit(solution)/shard_map/ppermute | solution.py:45
  37.2 0.0 copy-done.1
  37.2 0.1 reshape.38
  37.3 0.1 copy.8
  37.4 2.1 %collective-permute-done = bf16[1,4096]{1,0:T(2,128)(2,1)S(1)} collective-permute-done((bf16[1,4096]{1,0:T(2,128)(2,1)S(1)}, bf16[1,4096]{1,0:T(2,128)(2,1)S(1)}, u32[]{:S(2)}, u32[]{:S(2)}) %collective-permute-start) | collective-permute-done | bytes 8224 | tf_op jit(solution)/shard_map/ppermute | solution.py:45
  39.4 12.8 %fusion.14 = f32[2,4096]{1,0:T(2,128)S(1)} fusion(bf16[4096,4096]{1,0:T(8,128)(2,1)} %param.9, s32[]{:T(128)S(6)} %select_n.18, bf16[1,4096]{1,0:T(2,128)(2,1)S(1)} %collective-permute-done, bf16[1,4096]{1,0:T(2,128)(2,1)S(1)} %dynamic-slice_convert_fusion), kind=kOutput, calls=%fused_computation.15 | convolution fusion | flops 67174400 | bytes 33603588 | tf_op jit(solution)/shard_map/dot_general | solution.py:54
  52.3 15.8 %psum.22 = f32[2,4096]{1,0:T(2,128)S(1)} all-reduce(f32[2,4096]{1,0:T(2,128)S(1)} %fusion.14), channel_id=1, replica_groups=mesh['group'=2,'ctx'=4,'feat'=2,'ex'=2] {'ctx'}, use_global_device_ids=true, to_apply=%region_1.2 | all-reduce | flops 8192 | bytes 65536 | tf_op jit(solution)/shard_map/psum | solution.py:57
  68.0 0.1 multiply_reduce_fusion
  68.2 0.1 eq.18
  68.3 4.9 %psum.23 = f32[2]{0:T(128)S(1)} all-reduce(f32[2]{0:T(128)S(1)} %multiply_reduce_fusion), channel_id=1, replica_groups=mesh['group'=2,'ctx'=4,'feat'=2,'ex'=2] {'feat'}, use_global_device_ids=true, to_apply=%region_3.4 | all-reduce | flops 2 | bytes 16 | tf_op jit(solution)/shard_map/psum | solution.py:58
  73.2 0.1 divide_bitcast_fusion
  73.3 1.9 %all-gather = f32[2,2,4096]{2,1,0:T(2,128)S(1)} all-gather(f32[1,2,4096]{2,1,0:T(2,128)S(1)} %divide_bitcast_fusion), channel_id=1, replica_groups=mesh['group'=2,'ctx'=4,'feat'=2,'ex'=2] {'ex'}, dimensions={0}, use_global_device_ids=true | all-gather | bytes 98304 | tf_op jit(solution)/shard_map/all_gather | solution.py:60
  75.1 0.1 reshape.43
  75.2 0.9 %fusion.18 = f32[2,4096]{1,0:T(2,128)} fusion(f32[4,4096]{1,0:T(4,128)S(1)} %reshape.43, s32[4]{0:T(128)S(1)} %eq.18, s32[2]{0:T(128)S(1)} %iota_add_fusion), kind=kOutput, calls=%fused_computation.19 | convolution fusion | flops 393224 | bytes 98328 | tf_op jit(solution)/shard_map/dot_general | solution.py:67
  (4 shorter events, 0.0 us)
Async XLA Ops:
  0.0 1.6 %copy-start = (bf16[1,128,8192]{2,1,0:T(8,128)(2,1)S(1)}, bf16[1,128,8192]{2,1,0:T(8,128)(2,1)}, u32[]{:S(2)}) copy-start(bf16[1,128,8192]{2,1,0:T(8,128)(2,1)} %param.6) | copy-start | bytes 6291460
  0.0 37.2 %copy-start.1 = (s32[4]{0:T(128)S(1)}, s32[4]{0:T(128)}, u32[]{:S(2)}) copy-start(s32[4]{0:T(128)} %param.11) | copy-start | bytes 52
  35.6 3.8 %collective-permute-start = (bf16[1,4096]{1,0:T(2,128)(2,1)S(1)}, bf16[1,4096]{1,0:T(2,128)(2,1)S(1)}, u32[]{:S(2)}, u32[]{:S(2)}) collective-permute-start(bf16[1,4096]{1,0:T(2,128)(2,1)S(1)} %dynamic-slice_convert_fusion), channel_id=1, source_target_pairs={{0,2},{2,0},{1,3},{3,1},{4,6},{6,4},{5,7},{7,5},{8,10},{10,8},{9,1... | collective-permute-start | bytes 24584 | tf_op jit(solution)/shard_map/ppermute | solution.py:45
